TPU v7x, 512 devices: a whole 4x8x8 slice. The times are simulated.
512 devices in a mesh: space: 128 (over y_hi, x, z, core), filt: 4 (over y_lo).
Axes of the slice: x: 4, y: 8 (y_hi: 2, y_lo: 4; y = y_hi * 4 + y_lo), z: 8, core: 2. Of those that a mesh axis runs over, the one named last changes fastest.
Arguments:
- image: bfloat16 [96, 512, 1024], P(None, 'space', 'filt'), may hold values from -6 to 6
- cotangent: bfloat16 [96, 512, 1024], P(None, 'space', 'filt'), may hold values from -6 to 6
- kernel: float32 [96, 7, 7], replicated, may hold values from -0.875 to 0.875
- dw_bias: float32 [96], replicated, may hold values from -0.5 to 0.5
- layer_norm_gain: float32 [96], replicated, may hold values from 0.5 to 1.5
- layer_norm_bias: float32 [96], replicated, may hold values from -3 to 3
- w_expand: bfloat16 [384, 96], replicated, may hold values from -0.625 to 0.625
- b_expand: bfloat16 [384], replicated, may hold values from -3 to 3
- w_reduce: bfloat16 [384, 96], replicated, may hold values from -0.3125 to 0.3125
- b_reduce: float32 [96], replicated, may hold values from -3 to 3
- layer_scale: float32 [96], replicated, may hold values from 0.2 to 1
Outputs:
- output: bfloat16 [96, 512, 1024], P(None, 'space', 'filt')
- image_grad: bfloat16 [96, 512, 1024], P(None, 'space', 'filt')
- kernel_grad: float32 [96, 7, 7], replicated
- dw_bias_grad: float32 [96], replicated
- gain_grad: float32 [96], replicated
- ln_bias_grad: float32 [96], replicated
- expand_grad: float32 [384, 96], P('filt')
- expand_bias_grad: float32 [384], P('filt')
- reduce_grad: float32 [384, 96], P('filt')
- reduce_bias_grad: float32 [96], replicated
- scale_grad: float32 [96], replicated
All inputs are finite; a program needn't handle non-finite values.
Results may differ from a plain program's by a relative error of at most 0.011.
Values may be sent and summed in bfloat16 or wider, within the bound.
A program may use at most 64 MiB of HBM per device.

v0:
```python
import math
import jax
import jax.numpy as jnp
from jax import lax
from jax.sharding import PartitionSpec as P


def padded_2(x, sides, width):
    for axis, dim in sides:
        size, length = (lax.axis_size(axis), x.shape[dim])
        up = [(i, (i + 1) % size) for i in range(size - 1)]
        down = [(j, i) for i, j in up]
        last = lax.slice_in_dim(x, length - width, length, axis=dim)
        initial = lax.slice_in_dim(x, 0, width, axis=dim)
        before = lax.ppermute(last, axis, up)
        after = lax.ppermute(initial, axis, down)
        x = jnp.concatenate([before, x, after], axis=dim)
    return x


def depthwise(padded, kernel, row_count, col_count):
    total = jnp.zeros((padded.shape[0], row_count, col_count), jnp.float32)
    for shift_row in range(7):
        for shift_col in range(7):
            piece = padded[
                :, shift_row : shift_row + row_count, shift_col : shift_col + col_count
            ].astype(jnp.float32)
            total = total + kernel[:, shift_row, shift_col][:, None, None] * piece
    return total


def conv_back(padded, kernel, row_count, col_count):
    total = jnp.zeros((padded.shape[0], row_count, col_count), jnp.float32)
    for shift_row in range(7):
        for shift_col in range(7):
            piece = padded[
                :,
                6 - shift_row : 6 - shift_row + row_count,
                6 - shift_col : 6 - shift_col + col_count,
            ].astype(jnp.float32)
            total = total + kernel[:, shift_row, shift_col][:, None, None] * piece
    return total


def kernel_terms(padded, convolution_gradient, row_count, col_count):
    lines = []
    for shift_row in range(7):
        entries = []
        for shift_col in range(7):
            piece = padded[
                :, shift_row : shift_row + row_count, shift_col : shift_col + col_count
            ].astype(jnp.float32)
            entries.append(jnp.sum(piece * convolution_gradient, axis=(1, 2)))
        lines.append(jnp.stack(entries, axis=1))
    return jnp.stack(lines, axis=1)


def gelu_exact(value):
    return value * (1.0 + jax.scipy.special.erf(value / math.sqrt(2.0))) * 0.5


def gelu_slope(value):
    return (1.0 + jax.scipy.special.erf(value / math.sqrt(2.0))) * 0.5 + value * jnp.exp(
        -0.5 * value * value
    ) / math.sqrt(2.0 * math.pi)


def shards(
    image,
    cotangent,
    kernel,
    dw_bias,
    layer_norm_gain,
    layer_norm_bias,
    w_expand,
    b_expand,
    w_reduce,
    b_reduce,
    layer_scale,
):
    channels, row_count, col_count = image.shape
    panel_rows = w_expand.shape[0] // lax.axis_size("filt")
    tok_count = row_count * col_count
    padded = padded_2(image, (("space", 1), ("filt", 2)), 3)
    conv = depthwise(padded, kernel, row_count, col_count)
    conv = conv + dw_bias[:, None, None]
    flat = conv.reshape(channels, tok_count)
    average = jnp.mean(flat, axis=0, keepdims=True)
    mean_removed = flat - average
    inverse_deviation = lax.rsqrt(
        jnp.mean(mean_removed * mean_removed, axis=0, keepdims=True) + 1e-06
    )
    standardized_input = mean_removed * inverse_deviation
    normalized_input = (
        standardized_input * layer_norm_gain[:, None] + layer_norm_bias[:, None]
    ).astype(jnp.bfloat16)
    hidden = (
        jnp.dot(w_expand, normalized_input, preferred_element_type=jnp.float32)
        + b_expand.astype(jnp.float32)[:, None]
    )
    active = gelu_exact(hidden).astype(jnp.bfloat16)
    branch = (
        lax.dot_general(
            w_reduce, active, (((0,), (0,)), ((), ())), preferred_element_type=jnp.float32
        )
        + b_reduce[:, None]
    )
    resid = image.reshape(channels, tok_count).astype(jnp.float32)
    output = (
        (resid + layer_scale[:, None] * branch)
        .astype(jnp.bfloat16)
        .reshape(channels, row_count, col_count)
    )
    cot_flat = cotangent.reshape(channels, tok_count).astype(jnp.float32)
    scaled = layer_scale[:, None] * cot_flat
    g_scale = jnp.sum(cot_flat * branch, axis=1)
    g_rbias = jnp.sum(scaled, axis=1)
    d_branch = scaled.astype(jnp.bfloat16)
    g_reduce = lax.dot_general(
        active, d_branch, (((1,), (1,)), ((), ())), preferred_element_type=jnp.float32
    )
    d_active = jnp.dot(w_reduce, d_branch, preferred_element_type=jnp.float32)
    d_hidden = (d_active * gelu_slope(hidden)).astype(jnp.bfloat16)
    g_ebias = jnp.sum(d_hidden.astype(jnp.float32), axis=1)
    g_expand = lax.dot_general(
        d_hidden, normalized_input, (((1,), (1,)), ((), ())), preferred_element_type=jnp.float32
    )
    normalized_gradient = lax.dot_general(
        w_expand, d_hidden, (((0,), (0,)), ((), ())), preferred_element_type=jnp.float32
    )
    norm_gain_gradient = jnp.sum(normalized_gradient * standardized_input, axis=1)
    g_lbias = jnp.sum(normalized_gradient, axis=1)
    standardized_gradient = normalized_gradient * layer_norm_gain[:, None]
    convolution_gradient = inverse_deviation * (
        standardized_gradient
        - jnp.mean(standardized_gradient, axis=0, keepdims=True)
        - standardized_input
        * jnp.mean(standardized_gradient * standardized_input, axis=0, keepdims=True)
    )
    convolution_gradient = convolution_gradient.astype(jnp.bfloat16).reshape(
        channels, row_count, col_count
    )
    d_float = convolution_gradient.astype(jnp.float32)
    g_dbias = jnp.sum(d_float, axis=(1, 2))
    padded_grad = padded_2(convolution_gradient, (("space", 1), ("filt", 2)), 3)
    back = conv_back(padded_grad, kernel, row_count, col_count)
    image_grad = (cotangent.astype(jnp.float32) + back).astype(jnp.bfloat16)
    g_kernel = kernel_terms(padded, d_float, row_count, col_count)
    factor = 1.0 / math.sqrt(tok_count * lax.axis_size("space") * lax.axis_size("filt"))
    (
        g_reduce,
        g_expand,
        g_ebias,
        g_kernel,
        g_dbias,
        norm_gain_gradient,
        g_lbias,
        g_scale,
        g_rbias,
    ) = lax.psum(
        (
            g_reduce,
            g_expand,
            g_ebias,
            g_kernel,
            g_dbias,
            norm_gain_gradient,
            g_lbias,
            g_scale,
            g_rbias,
        ),
        ("space", "filt"),
    )
    start = lax.axis_index("filt") * panel_rows
    g_reduce = lax.dynamic_slice_in_dim(g_reduce, start, panel_rows, 0)
    g_expand = lax.dynamic_slice_in_dim(g_expand, start, panel_rows, 0)
    g_ebias = lax.dynamic_slice_in_dim(g_ebias, start, panel_rows, 0)
    return (
        output,
        image_grad,
        g_kernel * factor,
        g_dbias * factor,
        norm_gain_gradient * factor,
        g_lbias * factor,
        g_expand * factor,
        g_ebias * factor,
        g_reduce * factor,
        g_rbias * factor,
        g_scale * factor,
    )


def solution(mesh):
    in_specs = (
        P(None, "space", "filt"),
        P(None, "space", "filt"),
        P(),
        P(),
        P(),
        P(),
        P(),
        P(),
        P(),
        P(),
        P(),
    )
    out_specs = (
        P(None, "space", "filt"),
        P(None, "space", "filt"),
        P(),
        P(),
        P(),
        P(),
        P("filt", None),
        P("filt"),
        P("filt", None),
        P(),
        P(),
    )
    return jax.shard_map(shards, mesh=mesh, in_specs=in_specs, out_specs=out_specs, check_vma=False)
```

profile of v0, /device:TPU:1, one launch (start us, length us, event | category | flops | bytes accessed | tf_op | source)
XLA Modules:
  0.0 504.9 jit_solution(11829889516771855415)
XLA Ops:
  8.5 5.5 %collective-permute-start = (bf16[96,3,256]{2,1,0:T(4,128)(2,1)S(1)}, bf16[96,3,256]{2,1,0:T(4,128)(2,1)S(1)}, u32[]{:S(2)}, u32[]{:S(2)}) collective-permute-start(bf16[96,3,256]{2,1,0:T(4,128)(2,1)S(1)} %get-tuple-element.98), channel_id=1, source_target_pairs={{0,4},{4,8},{8,12},{12,16},{16,20},{20,24},{24,28},{28,32},{32,36}... | collective-permute-start | bytes 442376 | tf_op jit(solution)/shard_map/ppermute | solution.py:15
  14.0 4.7 collective-permute-start.1
  19.7 1.6 slice_bitcast_fusion.47
  21.5 1.5 slice_bitcast_fusion.46
  23.0 1.6 pad_maximum_fusion.2
  27.4 2.0 multiply_reduce_fusion.1
  30.5 6.1 %collective-permute-done.2 = bf16[96,10,3]{2,1,0:T(8,128)(2,1)S(1)} collective-permute-done((bf16[96,10,3]{2,1,0:T(8,128)(2,1)S(1)}, bf16[96,10,3]{2,1,0:T(8,128)(2,1)S(1)}, u32[]{:S(2)}, u32[]{:S(2)}) %collective-permute-start.2) | collective-permute-done | bytes 5792 | tf_op jit(solution)/shard_map/ppermute | solution.py:15
  37.4 1.5 collective-permute-done.3
  38.9 3.4 maximum_maximum_fusion
  42.7 11.5 %fusion.134 = (f32[4,256]{1,0:T(4,128)S(1)}, f32[96,4,256]{2,1,0:T(4,128)S(1)}) fusion(f32[96]{0:T(128)S(1)} %copy-done.92, bf16[96,10,259]{2,1,0:T(8,128)(2,1)S(1)} %get-tuple-element.93, f32[96]{0:T(128)S(1)} %copy-done.82, f32[96]{0:T(128)S(1)} %copy-done.84, f32[96]{0:T(128)S(1)} %get-tuple-element.101, ...), kind=kLoop, calls=%fused_computation.346 | loop fusion | flops 16317440 | bytes 9165568 | tf_op jit(solution)/shard_map/reduce_sum | solution.py:88
  54.6 1.5 fusion.9
  56.1 1.5 convert_reduce_fusion
  62.3 7.8 %fusion.115 = (f32[96]{0:T(128)}, f32[96]{0:T(128)}, f32[96]{0:T(128)}, f32[96]{0:T(128)}, f32[96]{0:T(128)}, /*index=5*/f32[96]{0:T(128)}, f32[96]{0:T(128)}, f...) fusion(bf16[96,4,256]{2,1,0:T(4,128)(2,1)S(1)} %reshape.89, ...), kind=kLoop, calls=%fused_computation.241 | loop fusion | flops 5404992 | bytes 3742464 | tf_op jit(solution)/shard_map/reduce_sum | solution.py:53
  70.0 9.8 %fusion.119 = (f32[96]{0:T(128)}, f32[96]{0:T(128)}, f32[96]{0:T(128)}, f32[96]{0:T(128)}, f32[96]{0:T(128)}, /*index=5*/f32[96]{0:T(128)}, f32[96]{0:T(128)}, f...) fusion(bf16[96,4,256]{2,1,0:T(4,128)(2,1)S(1)} %reshape.89, ...), kind=kLoop, calls=%fused_computation.245 | loop fusion | flops 5404992 | bytes 3742464 | tf_op jit(solution)/shard_map/reduce_sum | solution.py:53
  79.8 2.8 fusion.73
  84.7 5.9 %fusion.118 = (f32[96]{0:T(128)}, f32[96]{0:T(128)}, f32[96]{0:T(128)}, f32[96]{0:T(128)}, f32[96]{0:T(128)}, /*index=5*/f32[96]{0:T(128)}, f32[96]{0:T(128)}, f32[96]{0:T(128)}, f32[96]{0:T(128)}, f32[96]{0:T(128)}) fusion(bf16[96,4,256]{2,1,0:T(4,128)(2,1)S(1)} %reshape.89, bf16[96,10,259]{2,1,0:T(8,128)(2,1)S(1)} %get-tuple-element.93, ...), kind=kLoop, calls=%fused_computation.244 | loop fusion | flops 4815936 | bytes 1281792 | tf_op jit(solution)/shard_map/reduce_sum | solution.py:53
  97.4 108.8 %all-reduce = (f32[96,7,7]{0,2,1:T(8,128)S(1)}, f32[96]{0:T(128)S(1)}, f32[96]{0:T(128)S(1)}, f32[96]{0:T(128)S(1)}, f32[384]{0:T(512)S(1)}, /*index=5*/f32[96]{0:T(128)S(1)}, f32[96]{0:T(128)S(1)}) all-reduce(f32[96,7,7]{0,2,1:T(8,128)S(1)} %constant_dynamic-update-slice_fusion, ...), channel_id=1, replica_groups=mesh['space'=128,'filt'=4] {'space','filt'}, use_global_device_ids=true, to_apply=%region_53.0 | all-reduce | flops 5568 | bytes 44544 | tf_op jit(solution)/shard_map/psum | solution.py:160
  208.9 2.5 collective-permute-start.4
  211.4 1.9 collective-permute-start.5
  215.3 3.1 collective-permute-done.5
  220.4 4.0 collective-permute-start.7
  224.4 257.4 %all-reduce.4.cloned.1.call-done = (f32[384,96]{1,0:T(8,128)}, f32[384,96]{1,0:T(8,128)}) async-done(((f32[384,96]{1,0:T(8,128)}, f32[384,96]{1,0:T(8,128)}), (f32[384,96]{1,0:T(8,128)}, f32[384,96]{1,0:T(8,128)})) %all-reduce.4.cloned.1.call-update) | async-done | bytes 294928 | tf_op jit(solution)/shard_map/psum | solution.py:160
  483.7 2.3 pad_maximum_fusion.1
  486.3 11.7 %add_convert_fusion = bf16[96,4,256]{2,1,0:T(4,128)(2,1)} fusion(bf16[96,4,256]{2,1,0:T(4,128)(2,1)S(1)} %reshape.89, bf16[96,3,256]{2,1,0:T(4,128)(2,1)S(1)} %collective-permute-done.4, bf16[96,3,256]{2,1,0:T(4,128)(2,1)S(1)} %collective-permute-done.5, bf16[96,10,259]{2,1,0:T(8,128)(2,1)S(1)} %get-tuple-element.91, ...), kind=kLoop, calls=%fused_computation.252 | loop fusion | flops 16416768 | bytes 9161088 | tf_op jit(solution)/shard_map/convert_element_type | solution.py:147
  (242 shorter events, 28.7 us)
Async XLA Ops:
  7.2 47.4 %copy-start = (bf16[384,96]{0,1:T(8,128)(2,1)S(1)}, bf16[384,96]{0,1:T(8,128)(2,1)}, u32[]{:S(2)}) copy-start(bf16[384,96]{0,1:T(8,128)(2,1)} %param.17) | copy-start | bytes 221188
  7.2 474.7 %all-reduce.4.cloned.1.call-start = ((), (), s32[]{:S(2)}) async-start(), calls=%async_computation | async-start | bytes 786432 | tf_op jit(solution)/shard_map/psum | solution.py:160
  8.5 14.5 %collective-permute-start = (bf16[96,3,256]{2,1,0:T(4,128)(2,1)S(1)}, bf16[96,3,256]{2,1,0:T(4,128)(2,1)S(1)}, u32[]{:S(2)}, u32[]{:S(2)}) collective-permute-start(bf16[96,3,256]{2,1,0:T(4,128)(2,1)S(1)} %get-tuple-element.98), channel_id=1, source_target_pairs={{0,4},{4,8},{8,12},{12,16},{16,20},{20,24},{24,28},{28,32},{32,36}... | collective-permute-start | bytes 442376 | tf_op jit(solution)/shard_map/ppermute | solution.py:15
  14.0 9.0 %collective-permute-start.1 = (bf16[96,3,256]{2,1,0:T(4,128)(2,1)S(1)}, bf16[96,3,256]{2,1,0:T(4,128)(2,1)S(1)}, u32[]{:S(2)}, u32[]{:S(2)}) collective-permute-start(bf16[96,3,256]{2,1,0:T(4,128)(2,1)S(1)} %get-tuple-element.99), channel_id=1, source_target_pairs={{4,0},{8,4},{12,8},{16,12},{20,16},{24,20},{28,24},{32,28},{36,32}... | collective-permute-start | bytes 442376 | tf_op jit(solution)/shard_map/ppermute | solution.py:16
  19.7 22.7 %copy-start.16 = (f32[96]{0:T(128)}, f32[96]{0:T(128)S(1)}, u32[]{:S(2)}) copy-start(f32[96]{0:T(128)S(1)} %get-tuple-element.114) | copy-start | bytes 1156
  19.7 22.7 %copy-start.18 = (f32[96]{0:T(128)}, f32[96]{0:T(128)S(1)}, u32[]{:S(2)}) copy-start(f32[96]{0:T(128)S(1)} %get-tuple-element.115) | copy-start | bytes 1156
  19.7 22.7 %copy-start.20 = (f32[96]{0:T(128)}, f32[96]{0:T(128)S(1)}, u32[]{:S(2)}) copy-start(f32[96]{0:T(128)S(1)} %get-tuple-element.116) | copy-start | bytes 1156
  19.7 22.7 %copy-start.22 = (f32[96]{0:T(128)}, f32[96]{0:T(128)S(1)}, u32[]{:S(2)}) copy-start(f32[96]{0:T(128)S(1)} %get-tuple-element.117) | copy-start | bytes 1156
  19.7 22.7 %copy-start.24 = (f32[96]{0:T(128)}, f32[96]{0:T(128)S(1)}, u32[]{:S(2)}) copy-start(f32[96]{0:T(128)S(1)} %get-tuple-element.118) | copy-start | bytes 1156
  21.3 21.1 %copy-start.28 = (f32[96]{0:T(128)}, f32[96]{0:T(128)S(1)}, u32[]{:S(2)}) copy-start(f32[96]{0:T(128)S(1)} %get-tuple-element.120) | copy-start | bytes 1156
  21.3 21.1 %copy-start.30 = (f32[96]{0:T(128)}, f32[96]{0:T(128)S(1)}, u32[]{:S(2)}) copy-start(f32[96]{0:T(128)S(1)} %get-tuple-element.121) | copy-start | bytes 1156
  21.4 21.1 %copy-start.32 = (f32[96]{0:T(128)}, f32[96]{0:T(128)S(1)}, u32[]{:S(2)}) copy-start(f32[96]{0:T(128)S(1)} %get-tuple-element.122) | copy-start | bytes 1156
  21.4 21.1 %copy-start.34 = (f32[96]{0:T(128)}, f32[96]{0:T(128)S(1)}, u32[]{:S(2)}) copy-start(f32[96]{0:T(128)S(1)} %get-tuple-element.123) | copy-start | bytes 1156
  21.4 21.1 %copy-start.36 = (f32[96]{0:T(128)}, f32[96]{0:T(128)S(1)}, u32[]{:S(2)}) copy-start(f32[96]{0:T(128)S(1)} %get-tuple-element.124) | copy-start | bytes 1156
  21.4 21.1 %copy-start.38 = (f32[96]{0:T(128)}, f32[96]{0:T(128)S(1)}, u32[]{:S(2)}) copy-start(f32[96]{0:T(128)S(1)} %get-tuple-element.125) | copy-start | bytes 1156
  24.8 11.9 %collective-permute-start.2 = (bf16[96,10,3]{2,1,0:T(8,128)(2,1)S(1)}, bf16[96,10,3]{2,1,0:T(8,128)(2,1)S(1)}, u32[]{:S(2)}, u32[]{:S(2)}) collective-permute-start(bf16[96,10,3]{2,1,0:T(8,128)(2,1)S(1)} %get-tuple-element.88), channel_id=1, source_target_pairs={{0,1},{1,2},{2,3},{4,5},{5,6},{6,7},{8,9},{9,10},{10,11},{12,13},{... | collective-permute-start | bytes 17288 | tf_op jit(solution)/shard_map/ppermute | solution.py:15
  26.1 12.8 %collective-permute-start.3 = (bf16[96,10,3]{2,1,0:T(8,128)(2,1)S(1)}, bf16[96,10,3]{2,1,0:T(8,128)(2,1)}, u32[]{:S(2)}, u32[]{:S(2)}) collective-permute-start(bf16[96,10,3]{2,1,0:T(8,128)(2,1)S(1)} %get-tuple-element.89), channel_id=1, source_target_pairs={{1,0},{2,1},{3,2},{5,4},{6,5},{7,6},{9,8},{10,9},{11,10},{13,12},{... | collective-permute-start | bytes 17288 | tf_op jit(solution)/shard_map/ppermute | solution.py:16
  29.5 26.6 %copy-start.4 = (f32[12,8,4,256]{3,1,2,0:T(8,128)}, f32[12,8,4,256]{3,1,2,0:T(8,128)S(1)}, u32[]{:S(2)}) copy-start(f32[12,8,4,256]{3,1,2,0:T(8,128)S(1)} %copy.26) | copy-start | bytes 1179652
  90.6 118.3 %copy-start.12 = (bf16[96,3,256]{2,1,0:T(4,128)(2,1)S(1)}, bf16[96,3,256]{2,1,0:T(4,128)(2,1)}, u32[]{:S(2)}) copy-start(bf16[96,3,256]{2,1,0:T(4,128)(2,1)} %get-tuple-element.97) | copy-start | bytes 442372
  90.6 120.8 %copy-start.11 = (bf16[96,3,256]{2,1,0:T(4,128)(2,1)S(1)}, bf16[96,3,256]{2,1,0:T(4,128)(2,1)}, u32[]{:S(2)}) copy-start(bf16[96,3,256]{2,1,0:T(4,128)(2,1)} %get-tuple-element.96) | copy-start | bytes 442372
  208.9 6.4 %collective-permute-start.4 = (bf16[96,3,256]{2,1,0:T(4,128)(2,1)S(1)}, bf16[96,3,256]{2,1,0:T(4,128)(2,1)S(1)}, u32[]{:S(2)}, u32[]{:S(2)}) collective-permute-start(bf16[96,3,256]{2,1,0:T(4,128)(2,1)S(1)} %copy-done.12), channel_id=1, source_target_pairs={{0,4},{4,8},{8,12},{12,16},{16,20},{20,24},{24,28},{28,32},{32,36}... | collective-permute-start | bytes 442376 | tf_op jit(solution)/shard_map/ppermute | solution.py:15
  211.4 7.0 %collective-permute-start.5 = (bf16[96,3,256]{2,1,0:T(4,128)(2,1)S(1)}, bf16[96,3,256]{2,1,0:T(4,128)(2,1)S(1)}, u32[]{:S(2)}, u32[]{:S(2)}) collective-permute-start(bf16[96,3,256]{2,1,0:T(4,128)(2,1)S(1)} %copy-done.11), channel_id=1, source_target_pairs={{4,0},{8,4},{12,8},{16,12},{20,16},{24,20},{28,24},{32,28},{36,32}... | collective-permute-start | bytes 442376 | tf_op jit(solution)/shard_map/ppermute | solution.py:16
  219.1 264.6 %collective-permute-start.6 = (bf16[96,10,3]{2,1,0:T(8,128)(2,1)S(1)}, bf16[96,10,3]{2,1,0:T(8,128)(2,1)S(1)}, u32[]{:S(2)}, u32[]{:S(2)}) collective-permute-start(bf16[96,10,3]{2,1,0:T(8,128)(2,1)S(1)} %get-tuple-element.86), channel_id=1, source_target_pairs={{1,0},{2,1},{3,2},{5,4},{6,5},{7,6},{9,8},{10,9},{11,10},{13,12},{... | collective-permute-start | bytes 17288 | tf_op jit(solution)/shard_map/ppermute | solution.py:16
  220.4 263.3 %collective-permute-start.7 = (bf16[96,10,3]{2,1,0:T(8,128)(2,1)S(1)}, bf16[96,10,3]{2,1,0:T(8,128)(2,1)S(1)}, u32[]{:S(2)}, u32[]{:S(2)}) collective-permute-start(bf16[96,10,3]{2,1,0:T(8,128)(2,1)S(1)} %get-tuple-element.87), channel_id=1, source_target_pairs={{0,1},{1,2},{2,3},{4,5},{5,6},{6,7},{8,9},{9,10},{10,11},{12,13},{... | collective-permute-start | bytes 17288 | tf_op jit(solution)/shard_map/ppermute | solution.py:15
  (78 other events, 619.1 us)
Sparse Core Ops, SparseCore 0:
  214.8 266.9 all-reduce.3
where the time goes:
time: 506 us; the launch traced here: 505 us
  waiting for transfers between devices  268 us (53%)
  blocking collectives  109 us (22%)
  other arithmetic  66.2 us (13%)
  starting transfers between devices  22.6 us (4%)
  local copies, waits for them, and re-layouts  15.7 us (3%)
  between operations  15.6 us (3%)
  matrix products  7.76 us (2%)
    psum x1, waiting for transfers between devices, shards(): lax.psum((g_reduce, g_expand, g_ebias, g_kernel, g_dbias, norm_gain_gradi...  257 us
    psum x1, blocking collectives, shards(): lax.psum((g_reduce, g_expand, g_ebias, g_kernel, g_dbias, norm_gain_gradi...  109 us
    reduce_sum x4, other arithmetic, kernel_terms(): entries.append(jnp.sum(piece * convolution_gradient, axis=(1, 2)))  26.3 us
    ppermute x4, starting transfers between devices, padded_2(): before = lax.ppermute(last, axis, up)  13.4 us
    convert_element_type x1, other arithmetic, shards(): image_grad = (cotangent.astype(jnp.float32) + back).astype(jnp.bfloat16)  11.7 us
    reduce_sum x1, other arithmetic, shards(): average = jnp.mean(flat, axis=0, keepdims=True)  11.5 us
  transfers between devices with their start and end apart: 9, of which 4 were waited for; matrix products, arithmetic and copies ran while one was open for 2% of the time, Pallas kernels for 0%

commit v1 on v0

--- a/solution.py
+++ b/solution.py
@@ -158,18 +158,21 @@
         g_scale,
         g_rbias,
     ) = lax.psum(
-        (
-            g_reduce,
-            g_expand,
-            g_ebias,
-            g_kernel,
-            g_dbias,
-            norm_gain_gradient,
-            g_lbias,
-            g_scale,
-            g_rbias,
+        lax.psum(
+            (
+                g_reduce,
+                g_expand,
+                g_ebias,
+                g_kernel,
+                g_dbias,
+                norm_gain_gradient,
+                g_lbias,
+                g_scale,
+                g_rbias,
+            ),
+            "space",
         ),
-        ("space", "filt"),
+        "filt",
     )
     start = lax.axis_index("filt") * panel_rows
     g_reduce = lax.dynamic_slice_in_dim(g_reduce, start, panel_rows, 0)

time: 506 us -> 2450 us (4.84)
  waiting for transfers between devices: 268 us -> 1490 us
  blocking collectives: 109 us -> 812 us
    psum x1, waiting for transfers between devices: 257 us -> 1440 us  [shards(): lax.psum((g_reduce, g_expand, g_ebias, g_kernel, g_dbias, norm_gain_gradi...]
    psum x1, blocking collectives: 109 us -> 799 us  [shards(): lax.psum((g_reduce, g_expand, g_ebias, g_kernel, g_dbias, norm_gain_gradi...]
    psum x0 -> x1, waiting for transfers between devices: none -> 41.5 us  [shards(): lax.psum(lax.psum((g_reduce, g_expand, g_ebias, g_kernel, g_dbias, norm_g...]
  transfers between devices with their start and end apart: 9 -> 10, of which waited for: 4 -> 7; matrix products, arithmetic and copies ran while one was open for 2% -> 1% of each run, Pallas kernels for 0% -> 0%
where the time goes in v1:
time: 2450 us
  waiting for transfers between devices  1490 us (61%)
  blocking collectives  812 us (33%)
  other arithmetic  67.3 us (3%)
  starting transfers between devices  35.8 us (1%)
    psum x1, waiting for transfers between devices, shards(): lax.psum((g_reduce, g_expand, g_ebias, g_kernel, g_dbias, norm_gain_gradi...  1440 us
    psum x1, blocking collectives, shards(): lax.psum((g_reduce, g_expand, g_ebias, g_kernel, g_dbias, norm_gain_gradi...  799 us
  transfers between devices with their start and end apart: 10, of which 7 were waited for; matrix products, arithmetic and copies ran while one was open for 1% of the time, Pallas kernels for 0%

profile of v1, /device:TPU:1, one launch (start us, length us, event | category | flops | bytes accessed | tf_op | source)
XLA Modules:
  0.0 2449.1 jit_solution(17537007055685454712)
XLA Ops:
  8.5 5.5 collective-permute-start
  14.0 4.7 collective-permute-start.1
  19.7 1.6 slice_bitcast_fusion.47
  21.5 1.5 slice_bitcast_fusion.46
  23.0 1.6 pad_maximum_fusion.2
  27.4 2.0 multiply_reduce_fusion.1
  30.5 6.1 collective-permute-done.2
  37.4 1.5 collective-permute-done.3
  38.9 3.4 maximum_maximum_fusion
  42.7 11.5 fusion.134
  62.2 7.8 fusion.115
  70.0 9.8 fusion.119
  79.8 2.8 fusion.73
  84.7 5.9 fusion.118
  97.4 798.7 %all-reduce = (f32[96,7,7]{0,2,1:T(8,128)S(1)}, f32[96]{0:T(128)S(1)}, f32[96]{0:T(128)S(1)}, f32[96]{0:T(128)S(1)}, f32[384]{0:T(512)S(1)}, /*index=5*/f32[96]{0:T(128)S(1)}, f32[96]{0:T(128)S(1)}) all-reduce(f32[96,7,7]{0,2,1:T(8,128)S(1)} %constant_dynamic-update-slice_fusion, ...), channel_id=1, replica_groups=mesh['space'=128,'filt'=4] {'space'}, use_global_device_ids=true, to_apply=%region_53.0 | all-reduce | flops 5568 | bytes 44544 | tf_op jit(solution)/shard_map/psum | solution.py:161
  896.1 13.5 all-reduce.2
  912.3 6.8 collective-permute-start.4
  919.1 10.1 collective-permute-start.5
  932.2 4.7 collective-permute-start.7
  938.6 4.5 collective-permute-done.6
  944.0 3.4 pad_maximum_fusion.1
  947.4 1439.8 %all-reduce.7.cloned.1.call-done = (f32[384,96]{1,0:T(8,128)}, f32[384,96]{1,0:T(8,128)}) async-done(((f32[384,96]{1,0:T(8,128)}, f32[384,96]{1,0:T(8,128)}), (f32[384,96]{1,0:T(8,128)}, f32[384,96]{1,0:T(8,128)})) %all-reduce.7.cloned.1.call-update) | async-done | bytes 294928 | tf_op jit(solution)/shard_map/psum | solution.py:161
  2387.5 11.7 add_convert_fusion
  2399.2 41.5 %all-reduce.9.cloned.1.call-done = (f32[384,96]{1,0:T(8,128)}, f32[384,96]{1,0:T(8,128)}) async-done(((f32[384,96]{1,0:T(8,128)}, f32[384,96]{1,0:T(8,128)}), (f32[384,96]{1,0:T(8,128)}, f32[384,96]{1,0:T(8,128)})) %all-reduce.9.cloned.1.call-update) | async-done | bytes 294928 | tf_op jit(solution)/shard_map/psum | solution.py:160
  (248 shorter events, 33.1 us)
Async XLA Ops:
  7.2 2379.9 %all-reduce.7.cloned.1.call-start = ((), (), s32[]{:S(2)}) async-start(), calls=%async_computation | async-start | bytes 786432 | tf_op jit(solution)/shard_map/psum | solution.py:161
  8.5 14.5 collective-permute-start
  14.0 9.0 collective-permute-start.1
  24.8 11.9 collective-permute-start.2
  26.1 12.8 collective-permute-start.3
  912.3 17.4 collective-permute-start.4
  919.1 11.1 collective-permute-start.5
  929.1 1511.6 %all-reduce.9.cloned.1.call-start = ((), (), s32[]{:S(2)}) async-start(), calls=%async_computation.1 | async-start | bytes 786432 | tf_op jit(solution)/shard_map/psum | solution.py:160
  930.9 12.2 collective-permute-start.6
  932.2 11.8 collective-permute-start.7
  938.3 1448.9 %copy-start.24 = (f32[96]{0:T(128)S(1)}, f32[96]{0:T(128)}, u32[]{:S(2)}) copy-start(f32[96]{0:T(128)} %copy-done.23) | copy-start | bytes 1156
  938.3 1448.9 %copy-start.26 = (f32[96]{0:T(128)S(1)}, f32[96]{0:T(128)}, u32[]{:S(2)}) copy-start(f32[96]{0:T(128)} %copy-done.25) | copy-start | bytes 1156
  938.3 1448.9 %copy-start.28 = (f32[96]{0:T(128)S(1)}, f32[96]{0:T(128)}, u32[]{:S(2)}) copy-start(f32[96]{0:T(128)} %copy-done.27) | copy-start | bytes 1156
  938.3 1448.9 %copy-start.30 = (f32[96]{0:T(128)S(1)}, f32[96]{0:T(128)}, u32[]{:S(2)}) copy-start(f32[96]{0:T(128)} %copy-done.29) | copy-start | bytes 1156
  938.3 1448.9 %copy-start.32 = (f32[96]{0:T(128)S(1)}, f32[96]{0:T(128)}, u32[]{:S(2)}) copy-start(f32[96]{0:T(128)} %copy-done.31) | copy-start | bytes 1156
  938.4 1448.9 %copy-start.34 = (f32[96]{0:T(128)S(1)}, f32[96]{0:T(128)}, u32[]{:S(2)}) copy-start(f32[96]{0:T(128)} %copy-done.33) | copy-start | bytes 1156
  938.4 1448.9 %copy-start.36 = (f32[96]{0:T(128)S(1)}, f32[96]{0:T(128)}, u32[]{:S(2)}) copy-start(f32[96]{0:T(128)} %copy-done.35) | copy-start | bytes 1156
  938.4 1448.9 %copy-start.38 = (f32[96]{0:T(128)S(1)}, f32[96]{0:T(128)}, u32[]{:S(2)}) copy-start(f32[96]{0:T(128)} %copy-done.37) | copy-start | bytes 1156
  938.4 1448.9 %copy-start.40 = (f32[96]{0:T(128)S(1)}, f32[96]{0:T(128)}, u32[]{:S(2)}) copy-start(f32[96]{0:T(128)} %copy-done.39) | copy-start | bytes 1156
  938.4 1448.9 %copy-start.42 = (f32[96]{0:T(128)S(1)}, f32[96]{0:T(128)}, u32[]{:S(2)}) copy-start(f32[96]{0:T(128)} %copy-done.41) | copy-start | bytes 1156
  938.4 1448.9 %copy-start.44 = (f32[96]{0:T(128)S(1)}, f32[96]{0:T(128)}, u32[]{:S(2)}) copy-start(f32[96]{0:T(128)} %copy-done.43) | copy-start | bytes 1156
  938.4 1448.9 %copy-start.46 = (f32[96]{0:T(128)S(1)}, f32[96]{0:T(128)}, u32[]{:S(2)}) copy-start(f32[96]{0:T(128)} %copy-done.45) | copy-start | bytes 1156
  938.4 1448.9 %copy-start.48 = (f32[96]{0:T(128)S(1)}, f32[96]{0:T(128)}, u32[]{:S(2)}) copy-start(f32[96]{0:T(128)} %copy-done.47) | copy-start | bytes 1156
  938.4 1448.9 %copy-start.50 = (f32[96]{0:T(128)S(1)}, f32[96]{0:T(128)}, u32[]{:S(2)}) copy-start(f32[96]{0:T(128)} %copy-done.49) | copy-start | bytes 1156
  (80 other events, 34362.6 us)
Sparse Core Ops, SparseCore 0:
  929.3 1457.8 all-reduce.6
  2390.4 50.3 all-reduce.8
